TPU v7x, 32 devices: a whole 2x2x4 slice. The times are simulated.
32 devices in a mesh: grp: 8 (over z, core), row: 4 (over y, x).
Axes of the slice: x: 2, y: 2, z: 4, core: 2. Of those that a mesh axis runs over, the one named last changes fastest.
Arguments:
- theta: float32 [16, 512, 512], P('grp', 'row'), may hold values from -8 to 8
- left_env: bfloat16 [16, 8, 512, 512], P('grp', None, 'row'), may hold values from -1.5 to 1.5
- right_env: bfloat16 [16, 8, 512, 512], P('grp', None, 'row'), may hold values from -3.5 to 3.5
- lengths: int32 [16, 2], P('grp'), may hold values from 128 to 512
Outputs:
- evolved: float32 [16, 512, 512], P('grp', 'row')
- hessenberg: float32 [8, 8], replicated
All inputs are finite; a program needn't handle non-finite values.
Results may differ from a plain program's by a relative error of at most 0.0029.
Values may be sent and summed in bfloat16 or wider, within the bound.
A program may use at most 64 MiB of HBM per device.

v0:
```python
import jax
import jax.numpy as jnp
from jax import lax
from jax.sharding import PartitionSpec as P

KRYLOV = 8
epsilon = 1e-06
time_step = 0.5


def propagate(hessenberg):
    krylov_size = hessenberg.shape[0]
    scaled = time_step * hessenberg
    series = jnp.eye(krylov_size, dtype=jnp.float32)
    series_term = jnp.eye(krylov_size, dtype=jnp.float32)
    for degree in range(1, 19):
        series_term = jnp.dot(series_term, scaled, precision=lax.Precision.HIGHEST) / degree
        series = series + series_term
    return series[:, 0]


def local(theta, left_env, right_env, lengths):
    local_rows = theta.shape[1]
    sect_width = theta.shape[2]
    row_start = lax.axis_index("row") * local_rows
    row_ids = row_start + lax.broadcasted_iota(jnp.int32, (1, local_rows, 1), 1)
    col_ids = lax.broadcasted_iota(jnp.int32, (1, 1, sect_width), 2)
    live_mask = (
        (row_ids < lengths[:, 0][:, None, None]) & (col_ids < lengths[:, 1][:, None, None])
    ).astype(jnp.float32)
    right_full = lax.all_gather(right_env, "row", axis=2, tiled=True)
    start_block = theta * live_mask
    norm_zero = jnp.sqrt(lax.psum(jnp.sum(start_block * start_block), ("grp", "row")) + epsilon)
    krylov_basis = [start_block / norm_zero]
    krylov_size = KRYLOV
    hessenberg = jnp.zeros((krylov_size, krylov_size), jnp.float32)
    for column in range(krylov_size):
        packed = krylov_basis[column].astype(jnp.bfloat16)
        inner_terms = jnp.einsum(
            "sab,swbc->swac", packed, right_full, preferred_element_type=jnp.float32
        )
        inner_terms = inner_terms.astype(jnp.bfloat16)
        partial_image = jnp.einsum(
            "swba,swbc->sac", left_env, inner_terms, preferred_element_type=jnp.float32
        )
        image = lax.psum_scatter(partial_image, "row", scatter_dimension=1, tiled=True) * live_mask
        local_dots = jnp.stack([jnp.sum(vector * image) for vector in krylov_basis])
        coefficients, squared = lax.psum((local_dots, jnp.sum(image * image)), ("grp", "row"))
        for previous in range(column + 1):
            image = image - coefficients[previous] * krylov_basis[previous]
        hessenberg = hessenberg.at[: column + 1, column].set(coefficients)
        if column + 1 < krylov_size:
            beta_norm = jnp.sqrt(squared - jnp.sum(coefficients * coefficients) + epsilon)
            hessenberg = hessenberg.at[column + 1, column].set(beta_norm)
            krylov_basis.append(image / beta_norm)
    weights = propagate(hessenberg)
    evolved = jnp.zeros_like(start_block)
    for column in range(krylov_size):
        evolved = evolved + weights[column] * krylov_basis[column]
    return (norm_zero * evolved, hessenberg)


def solution(mesh):
    return jax.shard_map(
        local,
        mesh=mesh,
        in_specs=(
            P("grp", "row", None),
            P("grp", None, "row", None),
            P("grp", None, "row", None),
            P("grp", None),
        ),
        out_specs=(P("grp", "row", None), P()),
        check_vma=False,
    )
```

profile of v0, /device:TPU:0, one launch (start us, length us, event | category | flops | bytes accessed | tf_op | source)
XLA Modules:
  0.0 891.1 jit_solution(13568998900987345164)
XLA Ops:
  9.7 42.8 %psum.112 = f32[]{:T(128)} all-reduce(f32[]{:T(128)} %multiply_reduce_fusion.43), channel_id=1, replica_groups=mesh['grp'=8,'row'=4] {'grp','row'}, use_global_device_ids=true, to_apply=%region_1.0 | all-reduce | flops 1 | bytes 8 | tf_op jit(solution)/shard_map/psum | solution.py:33
  53.2 47.2 %all-gather.2.cloned.1.call-done = bf16[2,8,512,512]{3,2,1,0:T(8,128)(2,1)} async-done(((bf16[2,8,128,512]{3,2,1,0:T(8,128)(2,1)}), bf16[2,8,512,512]{3,2,1,0:T(8,128)(2,1)}) %all-gather.2.cloned.1.call-update) | async-done | bytes 8388624 | tf_op jit(solution)/shard_map/all_gather | solution.py:31
  100.4 8.9 fusion.24
  109.3 35.3 %reduce-scatter.9.cloned.1.call-done = f32[2,128,512]{1,2,0:T(8,128)} async-done(((f32[2,512,512]{1,2,0:T(8,128)}), f32[2,128,512]{1,2,0:T(8,128)}) %reduce-scatter.9.cloned.1.call-update) | async-done | bytes 524304 | tf_op jit(solution)/shard_map/reduce_scatter | solution.py:46
  146.5 39.5 %all-reduce.7 = (f32[]{:T(128)}, f32[1]{0:T(128)}) all-reduce(f32[]{:T(128)} %get-tuple-element.226, f32[1]{0:T(128)} %bitcast.6), channel_id=1, replica_groups=mesh['grp'=8,'row'=4] {'grp','row'}, use_global_device_ids=true, to_apply=%region_6.0 | all-reduce | flops 2 | bytes 16 | tf_op jit(solution)/shard_map/psum | solution.py:48
  189.9 8.7 fusion.29
  198.6 36.3 %reduce-scatter.11.cloned.1.call-done = f32[2,128,512]{1,2,0:T(8,128)} async-done(((f32[2,512,512]{1,2,0:T(8,128)}), f32[2,128,512]{1,2,0:T(8,128)}) %reduce-scatter.11.cloned.1.call-update) | async-done | bytes 524304 | tf_op jit(solution)/shard_map/reduce_scatter | solution.py:46
  238.1 39.6 %all-reduce.6 = (f32[]{:T(128)}, f32[2]{0:T(128)S(1)}) all-reduce(f32[]{:T(128)} %get-tuple-element.224, f32[2]{0:T(128)S(1)} %pad_maximum_fusion), channel_id=1, replica_groups=mesh['grp'=8,'row'=4] {'grp','row'}, use_global_device_ids=true, to_apply=%region_12.0 | all-reduce | flops 3 | bytes 24 | tf_op jit(solution)/shard_map/psum | solution.py:48
  283.5 8.9 fusion.34
  292.4 36.2 %reduce-scatter.13.cloned.1.call-done = f32[2,128,512]{1,2,0:T(8,128)} async-done(((f32[2,512,512]{1,2,0:T(8,128)}), f32[2,128,512]{1,2,0:T(8,128)}) %reduce-scatter.13.cloned.1.call-update) | async-done | bytes 524304 | tf_op jit(solution)/shard_map/reduce_scatter | solution.py:46
  332.8 39.5 %all-reduce.5 = (f32[]{:T(128)}, f32[3]{0:T(128)S(1)}) all-reduce(f32[]{:T(128)} %get-tuple-element.221, f32[3]{0:T(128)S(1)} %pad_maximum_fusion.1), channel_id=1, replica_groups=mesh['grp'=8,'row'=4] {'grp','row'}, use_global_device_ids=true, to_apply=%region_21.0 | all-reduce | flops 4 | bytes 32 | tf_op jit(solution)/shard_map/psum | solution.py:48
  378.9 8.9 fusion.39
  387.9 36.3 %reduce-scatter.15.cloned.1.call-done = f32[2,128,512]{1,2,0:T(8,128)} async-done(((f32[2,512,512]{1,2,0:T(8,128)}), f32[2,128,512]{1,2,0:T(8,128)}) %reduce-scatter.15.cloned.1.call-update) | async-done | bytes 524304 | tf_op jit(solution)/shard_map/reduce_scatter | solution.py:46
  429.0 39.7 %all-reduce.4 = (f32[]{:T(128)}, f32[4]{0:T(128)S(1)}) all-reduce(f32[]{:T(128)} %get-tuple-element.217, f32[4]{0:T(128)S(1)} %pad_maximum_fusion.2), channel_id=1, replica_groups=mesh['grp'=8,'row'=4] {'grp','row'}, use_global_device_ids=true, to_apply=%region_31.0 | all-reduce | flops 5 | bytes 40 | tf_op jit(solution)/shard_map/psum | solution.py:48
  471.2 5.1 subtract_divide_fusion.3
  476.2 8.9 fusion.44
  485.2 36.2 %reduce-scatter.17.cloned.1.call-done = f32[2,128,512]{1,2,0:T(8,128)} async-done(((f32[2,512,512]{1,2,0:T(8,128)}), f32[2,128,512]{1,2,0:T(8,128)}) %reduce-scatter.17.cloned.1.call-update) | async-done | bytes 524304 | tf_op jit(solution)/shard_map/reduce_scatter | solution.py:46
  527.1 39.5 %all-reduce.3 = (f32[]{:T(128)}, f32[5]{0:T(128)S(1)}) all-reduce(f32[]{:T(128)} %get-tuple-element.211, f32[5]{0:T(128)S(1)} %stack.147), channel_id=1, replica_groups=mesh['grp'=8,'row'=4] {'grp','row'}, use_global_device_ids=true, to_apply=%region_42.0 | all-reduce | flops 6 | bytes 48 | tf_op jit(solution)/shard_map/psum | solution.py:48
  569.2 5.8 subtract_divide_fusion.2
  575.1 8.9 fusion.49
  584.0 36.3 %reduce-scatter.19.cloned.1.call-done = f32[2,128,512]{1,2,0:T(8,128)} async-done(((f32[2,512,512]{1,2,0:T(8,128)}), f32[2,128,512]{1,2,0:T(8,128)}) %reduce-scatter.19.cloned.1.call-update) | async-done | bytes 524304 | tf_op jit(solution)/shard_map/reduce_scatter | solution.py:46
  626.9 39.9 %all-reduce.2 = (f32[]{:T(128)}, f32[6]{0:T(128)S(1)}) all-reduce(f32[]{:T(128)} %get-tuple-element.205, f32[6]{0:T(128)S(1)} %stack.154), channel_id=1, replica_groups=mesh['grp'=8,'row'=4] {'grp','row'}, use_global_device_ids=true, to_apply=%region_54.0 | all-reduce | flops 7 | bytes 56 | tf_op jit(solution)/shard_map/psum | solution.py:48
  669.4 6.6 subtract_divide_fusion.1
  676.0 8.9 fusion.54
  684.9 36.3 %reduce-scatter.21.cloned.1.call-done = f32[2,128,512]{1,2,0:T(8,128)} async-done(((f32[2,512,512]{1,2,0:T(8,128)}), f32[2,128,512]{1,2,0:T(8,128)}) %reduce-scatter.21.cloned.1.call-update) | async-done | bytes 524304 | tf_op jit(solution)/shard_map/reduce_scatter | solution.py:46
  728.7 39.5 %all-reduce.1 = (f32[]{:T(128)}, f32[7]{0:T(128)S(1)}) all-reduce(f32[]{:T(128)} %get-tuple-element.198, f32[7]{0:T(128)S(1)} %stack.162), channel_id=1, replica_groups=mesh['grp'=8,'row'=4] {'grp','row'}, use_global_device_ids=true, to_apply=%region_67.0 | all-reduce | flops 8 | bytes 64 | tf_op jit(solution)/shard_map/psum | solution.py:48
  770.8 7.3 subtract_divide_fusion
  778.1 8.9 fusion.59
  815.2 8.2 reduce-scatter.23.cloned.1.call-done
  826.5 5.1 stack.171
  831.8 39.3 %psum.127 = f32[8,1]{1,0:T(8,128)S(1)} all-reduce(f32[8,1]{1,0:T(8,128)S(1)} %copy.13), channel_id=1, replica_groups=mesh['grp'=8,'row'=4] {'grp','row'}, use_global_device_ids=true, to_apply=%region_78.0 | all-reduce | flops 8 | bytes 64 | tf_op jit(solution)/shard_map/psum | solution.py:48
  874.3 8.0 add_multiply_fusion
  (135 shorter events, 90.3 us)
Async XLA Ops:
  7.2 93.2 %copy-start = (bf16[2,8,128,512]{3,2,1,0:T(8,128)(2,1)S(1)}, bf16[2,8,128,512]{3,2,1,0:T(8,128)(2,1)}, u32[]{:S(2)}) copy-start(bf16[2,8,128,512]{3,2,1,0:T(8,128)(2,1)} %param.35) | copy-start | bytes 6291460
  7.2 1.2 copy-start.2
  7.2 1.4 copy-start.3
  7.2 93.2 %all-gather.2.cloned.1.call-start = ((), (), s32[]{:S(2)}) async-start(), calls=%async_computation.8 | async-start | bytes 10485760 | tf_op jit(solution)/shard_map/all_gather | solution.py:31
  7.9 136.7 %reduce-scatter.9.cloned.1.call-start = ((), (), s32[]{:S(2)}) async-start(), calls=%async_computation.9 | async-start | bytes 2621440 | tf_op jit(solution)/shard_map/reduce_scatter | solution.py:46
  109.3 125.6 %reduce-scatter.11.cloned.1.call-start = ((), (), s32[]{:S(2)}) async-start(), calls=%async_computation.10 | async-start | bytes 2621440 | tf_op jit(solution)/shard_map/reduce_scatter | solution.py:46
  198.6 130.0 %reduce-scatter.13.cloned.1.call-start = ((), (), s32[]{:S(2)}) async-start(), calls=%async_computation.11 | async-start | bytes 2621440 | tf_op jit(solution)/shard_map/reduce_scatter | solution.py:46
  292.4 131.8 %reduce-scatter.15.cloned.1.call-start = ((), (), s32[]{:S(2)}) async-start(), calls=%async_computation.12 | async-start | bytes 2621440 | tf_op jit(solution)/shard_map/reduce_scatter | solution.py:46
  387.8 133.6 %reduce-scatter.17.cloned.1.call-start = ((), (), s32[]{:S(2)}) async-start(), calls=%async_computation.13 | async-start | bytes 2621440 | tf_op jit(solution)/shard_map/reduce_scatter | solution.py:46
  485.1 135.2 %reduce-scatter.19.cloned.1.call-start = ((), (), s32[]{:S(2)}) async-start(), calls=%async_computation.14 | async-start | bytes 2621440 | tf_op jit(solution)/shard_map/reduce_scatter | solution.py:46
  584.0 137.3 %reduce-scatter.21.cloned.1.call-start = ((), (), s32[]{:S(2)}) async-start(), calls=%async_computation.15 | async-start | bytes 2621440 | tf_op jit(solution)/shard_map/reduce_scatter | solution.py:46
  684.9 138.5 %reduce-scatter.23.cloned.1.call-start = ((), (), s32[]{:S(2)}) async-start(), calls=%async_computation.16 | async-start | bytes 2621440 | tf_op jit(solution)/shard_map/reduce_scatter | solution.py:46
  787.0 3.8 copy-start.8
  787.0 4.5 copy-start.7
  787.0 5.2 copy-start.6
  787.0 5.9 copy-start.5
  787.0 6.6 copy-start.4
  871.2 11.2 %copy-start.1 = (f32[8,8]{1,0:T(8,128)}, f32[8,8]{1,0:T(8,128)S(1)}, u32[]{:S(2)}) copy-start(f32[8,8]{1,0:T(8,128)S(1)} %scatter.74) | copy-start | bytes 772
Sparse Core Ops, SparseCore 0:
  9.9 90.4 all-gather.1
  109.4 35.1 reduce-scatter.8
  198.7 36.1 reduce-scatter.10
  292.5 36.1 reduce-scatter.12
  387.9 36.1 reduce-scatter.14
  485.3 36.0 reduce-scatter.16
  584.1 36.1 reduce-scatter.18
  685.0 36.2 reduce-scatter.20
  787.1 36.2 reduce-scatter.22
where the time goes:
time: 901 us; the launch traced here: 891 us
  blocking collectives  359 us (40%)
  waiting for transfers between devices  309 us (34%)
  other arithmetic  85.4 us (9%)
  matrix products  73.3 us (8%)
  local copies, waits for them, and re-layouts  39 us (4%)
  between operations  24.8 us (3%)
    psum x8, blocking collectives, local(): lax.psum((local_dots, jnp.sum(image * image)), ('grp', 'row'))  316 us
    reduce_scatter x8, waiting for transfers between devices, local(): lax.psum_scatter(partial_image, 'row', scatter_dimension=1, tiled=True)  261 us
    dot_general x8, matrix products, local(): jnp.einsum('swba,swbc->sac', left_env, inner_terms, preferred_element_typ...  70.8 us
    all_gather x1, waiting for transfers between devices, local(): right_full = lax.all_gather(right_env, 'row', axis=2, tiled=True)  47.2 us
    psum x1, blocking collectives, local(): lax.psum(jnp.sum(start_block * start_block), ('grp', 'row')) + epsilon  42.8 us
    div x7, other arithmetic, local(): krylov_basis.append(image / beta_norm)  34 us
    reduce_sum x8, other arithmetic, local(): local_dots = jnp.stack([jnp.sum(vector * image) for vector in krylov_basis])  19.7 us
  transfers between devices with their start and end apart: 9, of which 9 were waited for; matrix products, arithmetic and copies ran while one was open for 3% of the time, Pallas kernels for 0%

commit v1 on v0

--- a/solution.py
+++ b/solution.py
@@ -1,3 +1,4 @@
+import functools
 import jax
 import jax.numpy as jnp
 from jax import lax
@@ -6,6 +7,15 @@
 KRYLOV = 8
 epsilon = 1e-06
 time_step = 0.5
+
+
+def _number_forms(vals, shard_axis, along_axis):
+    for tick in (shard_axis, along_axis):
+        vals = lax.psum(vals, axis_name=tick)
+    return vals
+
+
+review_the_heaps = functools.partial(_number_forms, shard_axis="row", along_axis="grp")
 
 
 def propagate(hessenberg):
@@ -45,7 +55,7 @@
         )
         image = lax.psum_scatter(partial_image, "row", scatter_dimension=1, tiled=True) * live_mask
         local_dots = jnp.stack([jnp.sum(vector * image) for vector in krylov_basis])
-        coefficients, squared = lax.psum((local_dots, jnp.sum(image * image)), ("grp", "row"))
+        coefficients, squared = review_the_heaps((local_dots, jnp.sum(image * image)))
         for previous in range(column + 1):
             image = image - coefficients[previous] * krylov_basis[previous]
         hessenberg = hessenberg.at[: column + 1, column].set(coefficients)

time: 901 us -> 754 us (0.84)
  blocking collectives: 359 us -> 237 us
  waiting for transfers between devices: 309 us -> 284 us
    psum x8 -> x16, blocking collectives: 316 us -> 195 us  [_number_forms(): vals = lax.psum(vals, axis_name=tick)]
    reduce_scatter x8, waiting for transfers between devices: 261 us -> 236 us  [local(): lax.psum_scatter(partial_image, 'row', scatter_dimension=1, tiled=True)]
  transfers between devices with their start and end apart: 9 -> 9, of which waited for: 9 -> 9; matrix products, arithmetic and copies ran while one was open for 3% -> 4% of each run, Pallas kernels for 0% -> 0%
where the time goes in v1:
time: 754 us; the launch traced here: 745 us
  waiting for transfers between devices  284 us (38%)
  blocking collectives  237 us (31%)
  other arithmetic  85.6 us (11%)
  matrix products  73.3 us (10%)
  local copies, waits for them, and re-layouts  39.4 us (5%)
  between operations  24.9 us (3%)
    reduce_scatter x8, waiting for transfers between devices, local(): lax.psum_scatter(partial_image, 'row', scatter_dimension=1, tiled=True)  236 us
    psum x16, blocking collectives, _number_forms(): vals = lax.psum(vals, axis_name=tick)  195 us
    dot_general x8, matrix products, local(): jnp.einsum('swba,swbc->sac', left_env, inner_terms, preferred_element_typ...  70.8 us
    all_gather x1, waiting for transfers between devices, local(): right_full = lax.all_gather(right_env, 'row', axis=2, tiled=True)  47.1 us
    psum x1, blocking collectives, local(): lax.psum(jnp.sum(start_block * start_block), ('grp', 'row')) + epsilon  42.8 us
    div x7, other arithmetic, local(): krylov_basis.append(image / beta_norm)  34 us
    reduce_sum x8, other arithmetic, local(): local_dots = jnp.stack([jnp.sum(vector * image) for vector in krylov_basis])  19.7 us
    another operation x4, local copies, waits for them, and re-layouts, local(): local_dots = jnp.stack([jnp.sum(vector * image) for vector in krylov_basis])  16.7 us
  transfers between devices with their start and end apart: 9, of which 9 were waited for; matrix products, arithmetic and copies ran while one was open for 4% of the time, Pallas kernels for 0%

profile of v1, /device:TPU:0, one launch (start us, length us, event | category | flops | bytes accessed | tf_op | source)
XLA Modules:
  0.0 745.0 jit_solution(268175293814711863)
XLA Ops:
  9.7 42.8 %psum.217 = f32[]{:T(128)} all-reduce(f32[]{:T(128)} %multiply_reduce_fusion.43), channel_id=1, replica_groups=mesh['grp'=8,'row'=4] {'grp','row'}, use_global_device_ids=true, to_apply=%region_1.0 | all-reduce | flops 1 | bytes 8 | tf_op jit(solution)/shard_map/psum | solution.py:43
  53.2 47.1 %all-gather.2.cloned.1.call-done = bf16[2,8,512,512]{3,2,1,0:T(8,128)(2,1)} async-done(((bf16[2,8,128,512]{3,2,1,0:T(8,128)(2,1)}), bf16[2,8,512,512]{3,2,1,0:T(8,128)(2,1)}) %all-gather.2.cloned.1.call-update) | async-done | bytes 8388624 | tf_op jit(solution)/shard_map/all_gather | solution.py:41
  100.4 8.9 %fusion.24 = f32[2,512,512]{1,2,0:T(8,128)} fusion(bf16[2,8,128,512]{3,2,1,0:T(8,128)(2,1)S(1)} %copy-done, bf16[2,8,512,512]{3,2,1,0:T(8,128)(2,1)} %all-gather.2.cloned.1.call-done, f32[2,128,512]{1,2,0:T(8,128)S(1)} %copy.6, f32[]{:T(128)S(6)} %sqrt.24, pred[2,512]{1,0:T(4,128)(4,1)S(1)} %iota_compare_fusion.2, pred[2,128]{1,0:T(4,128)(4,1)S(1)} %broadcast_compare_fusion), kind=kOutput, calls=%fused_computation.24 | convolution fusion | flops 2149056512 | bytes 13108484 | tf_op jit(solution)/shard_map/swba,swbc->sac/dot_general | solution.py:53
  109.3 35.3 %reduce-scatter.9.cloned.1.call-done = f32[2,128,512]{1,2,0:T(8,128)} async-done(((f32[2,512,512]{1,2,0:T(8,128)}), f32[2,128,512]{1,2,0:T(8,128)}) %reduce-scatter.9.cloned.1.call-update) | async-done | bytes 524304 | tf_op jit(solution)/shard_map/reduce_scatter | solution.py:56
  146.5 9.5 %all-reduce.14 = (f32[]{:T(128)}, f32[1]{0:T(128)}) all-reduce(f32[]{:T(128)} %get-tuple-element.226, f32[1]{0:T(128)} %bitcast.6), channel_id=1, replica_groups=mesh['grp'=8,'row'=4] {'row'}, use_global_device_ids=true, to_apply=%region_7.0 | all-reduce | flops 2 | bytes 16 | tf_op jit(solution)/shard_map/psum | solution.py:14
  156.0 14.8 %all-reduce.7 = (f32[]{:T(128)}, f32[1]{0:T(128)}) all-reduce(f32[]{:T(128)} %get-tuple-element.255, f32[1]{0:T(128)} %get-tuple-element.256), channel_id=1, replica_groups=mesh['grp'=8,'row'=4] {'grp'}, use_global_device_ids=true, to_apply=%region_8.0 | all-reduce | flops 2 | bytes 16 | tf_op jit(solution)/shard_map/psum | solution.py:14
  183.5 32.5 %reduce-scatter.11.cloned.1.call-done = f32[2,128,512]{1,2,0:T(8,128)} async-done(((f32[2,512,512]{1,2,0:T(8,128)}), f32[2,128,512]{1,2,0:T(8,128)}) %reduce-scatter.11.cloned.1.call-update) | async-done | bytes 524304 | tf_op jit(solution)/shard_map/reduce_scatter | solution.py:56
  219.2 9.5 %all-reduce.13 = (f32[]{:T(128)}, f32[2]{0:T(128)S(1)}) all-reduce(f32[]{:T(128)} %get-tuple-element.224, f32[2]{0:T(128)S(1)} %pad_maximum_fusion), channel_id=1, replica_groups=mesh['grp'=8,'row'=4] {'row'}, use_global_device_ids=true, to_apply=%region_15.0 | all-reduce | flops 3 | bytes 24 | tf_op jit(solution)/shard_map/psum | solution.py:14
  228.7 15.3 %all-reduce.6 = (f32[]{:T(128)}, f32[2]{0:T(128)S(1)}) all-reduce(f32[]{:T(128)} %get-tuple-element.253, f32[2]{0:T(128)S(1)} %get-tuple-element.254), channel_id=1, replica_groups=mesh['grp'=8,'row'=4] {'grp'}, use_global_device_ids=true, to_apply=%region_16.0 | all-reduce | flops 3 | bytes 24 | tf_op jit(solution)/shard_map/psum | solution.py:14
  249.8 8.9 %fusion.34 = f32[2,512,512]{1,2,0:T(8,128)} fusion(bf16[2,8,128,512]{3,2,1,0:T(8,128)(2,1)S(1)} %copy-done, bf16[2,8,512,512]{3,2,1,0:T(8,128)(2,1)} %all-gather.2.cloned.1.call-done, f32[2,128,512]{1,2,0:T(8,128)} %subtract_divide_fusion.5), kind=kOutput, calls=%fused_computation.28 | convolution fusion | flops 2148663296 | bytes 13107200 | tf_op jit(solution)/shard_map/swba,swbc->sac/dot_general | solution.py:53
  258.7 32.5 %reduce-scatter.13.cloned.1.call-done = f32[2,128,512]{1,2,0:T(8,128)} async-done(((f32[2,512,512]{1,2,0:T(8,128)}), f32[2,128,512]{1,2,0:T(8,128)}) %reduce-scatter.13.cloned.1.call-update) | async-done | bytes 524304 | tf_op jit(solution)/shard_map/reduce_scatter | solution.py:56
  295.4 9.6 %all-reduce.12 = (f32[]{:T(128)}, f32[3]{0:T(128)S(1)}) all-reduce(f32[]{:T(128)} %get-tuple-element.221, f32[3]{0:T(128)S(1)} %pad_maximum_fusion.1), channel_id=1, replica_groups=mesh['grp'=8,'row'=4] {'row'}, use_global_device_ids=true, to_apply=%region_26.0 | all-reduce | flops 4 | bytes 32 | tf_op jit(solution)/shard_map/psum | solution.py:14
  305.0 14.8 %all-reduce.5 = (f32[]{:T(128)}, f32[3]{0:T(128)S(1)}) all-reduce(f32[]{:T(128)} %get-tuple-element.251, f32[3]{0:T(128)S(1)} %get-tuple-element.252), channel_id=1, replica_groups=mesh['grp'=8,'row'=4] {'grp'}, use_global_device_ids=true, to_apply=%region_27.0 | all-reduce | flops 4 | bytes 32 | tf_op jit(solution)/shard_map/psum | solution.py:14
  326.5 8.9 %fusion.39 = f32[2,512,512]{1,2,0:T(8,128)} fusion(bf16[2,8,128,512]{3,2,1,0:T(8,128)(2,1)S(1)} %copy-done, bf16[2,8,512,512]{3,2,1,0:T(8,128)(2,1)} %all-gather.2.cloned.1.call-done, f32[2,128,512]{1,2,0:T(8,128)} %subtract_divide_fusion.4), kind=kOutput, calls=%fused_computation.30 | convolution fusion | flops 2148663296 | bytes 13107200 | tf_op jit(solution)/shard_map/swba,swbc->sac/dot_general | solution.py:53
  335.5 32.5 %reduce-scatter.15.cloned.1.call-done = f32[2,128,512]{1,2,0:T(8,128)} async-done(((f32[2,512,512]{1,2,0:T(8,128)}), f32[2,128,512]{1,2,0:T(8,128)}) %reduce-scatter.15.cloned.1.call-update) | async-done | bytes 524304 | tf_op jit(solution)/shard_map/reduce_scatter | solution.py:56
  372.9 9.6 %all-reduce.11 = (f32[]{:T(128)}, f32[4]{0:T(128)S(1)}) all-reduce(f32[]{:T(128)} %get-tuple-element.217, f32[4]{0:T(128)S(1)} %pad_maximum_fusion.2), channel_id=1, replica_groups=mesh['grp'=8,'row'=4] {'row'}, use_global_device_ids=true, to_apply=%region_38.0 | all-reduce | flops 5 | bytes 40 | tf_op jit(solution)/shard_map/psum | solution.py:14
  382.5 14.9 %all-reduce.4 = (f32[]{:T(128)}, f32[4]{0:T(128)S(1)}) all-reduce(f32[]{:T(128)} %get-tuple-element.249, f32[4]{0:T(128)S(1)} %get-tuple-element.250), channel_id=1, replica_groups=mesh['grp'=8,'row'=4] {'grp'}, use_global_device_ids=true, to_apply=%region_39.0 | all-reduce | flops 5 | bytes 40 | tf_op jit(solution)/shard_map/psum | solution.py:14
  405.0 8.9 %fusion.44 = f32[2,512,512]{1,2,0:T(8,128)} fusion(bf16[2,8,128,512]{3,2,1,0:T(8,128)(2,1)S(1)} %copy-done, bf16[2,8,512,512]{3,2,1,0:T(8,128)(2,1)} %all-gather.2.cloned.1.call-done, f32[2,128,512]{1,2,0:T(8,128)} %subtract_divide_fusion.3), kind=kOutput, calls=%fused_computation.32 | convolution fusion | flops 2148663296 | bytes 13107200 | tf_op jit(solution)/shard_map/swba,swbc->sac/dot_general | solution.py:53
  413.9 32.5 %reduce-scatter.17.cloned.1.call-done = f32[2,128,512]{1,2,0:T(8,128)} async-done(((f32[2,512,512]{1,2,0:T(8,128)}), f32[2,128,512]{1,2,0:T(8,128)}) %reduce-scatter.17.cloned.1.call-update) | async-done | bytes 524304 | tf_op jit(solution)/shard_map/reduce_scatter | solution.py:56
  452.2 9.6 %all-reduce.10 = (f32[]{:T(128)}, f32[5]{0:T(128)S(1)}) all-reduce(f32[]{:T(128)} %get-tuple-element.211, f32[5]{0:T(128)S(1)} %stack.147), channel_id=1, replica_groups=mesh['grp'=8,'row'=4] {'row'}, use_global_device_ids=true, to_apply=%region_51.0 | all-reduce | flops 6 | bytes 48 | tf_op jit(solution)/shard_map/psum | solution.py:14
  461.8 14.8 %all-reduce.3 = (f32[]{:T(128)}, f32[5]{0:T(128)S(1)}) all-reduce(f32[]{:T(128)} %get-tuple-element.247, f32[5]{0:T(128)S(1)} %get-tuple-element.248), channel_id=1, replica_groups=mesh['grp'=8,'row'=4] {'grp'}, use_global_device_ids=true, to_apply=%region_52.0 | all-reduce | flops 6 | bytes 48 | tf_op jit(solution)/shard_map/psum | solution.py:14
  485.1 8.9 %fusion.49 = f32[2,512,512]{1,2,0:T(8,128)} fusion(bf16[2,8,128,512]{3,2,1,0:T(8,128)(2,1)S(1)} %copy-done, bf16[2,8,512,512]{3,2,1,0:T(8,128)(2,1)} %all-gather.2.cloned.1.call-done, f32[2,128,512]{1,2,0:T(8,128)} %subtract_divide_fusion.2), kind=kOutput, calls=%fused_computation.34 | convolution fusion | flops 2148663296 | bytes 13107200 | tf_op jit(solution)/shard_map/swba,swbc->sac/dot_general | solution.py:53
  494.0 32.5 %reduce-scatter.19.cloned.1.call-done = f32[2,128,512]{1,2,0:T(8,128)} async-done(((f32[2,512,512]{1,2,0:T(8,128)}), f32[2,128,512]{1,2,0:T(8,128)}) %reduce-scatter.19.cloned.1.call-update) | async-done | bytes 524304 | tf_op jit(solution)/shard_map/reduce_scatter | solution.py:56
  533.2 9.6 %all-reduce.9 = (f32[]{:T(128)}, f32[6]{0:T(128)S(1)}) all-reduce(f32[]{:T(128)} %get-tuple-element.205, f32[6]{0:T(128)S(1)} %stack.154), channel_id=1, replica_groups=mesh['grp'=8,'row'=4] {'row'}, use_global_device_ids=true, to_apply=%region_65.0 | all-reduce | flops 7 | bytes 56 | tf_op jit(solution)/shard_map/psum | solution.py:14
  542.8 15.1 %all-reduce.2 = (f32[]{:T(128)}, f32[6]{0:T(128)S(1)}) all-reduce(f32[]{:T(128)} %get-tuple-element.245, f32[6]{0:T(128)S(1)} %get-tuple-element.246), channel_id=1, replica_groups=mesh['grp'=8,'row'=4] {'grp'}, use_global_device_ids=true, to_apply=%region_66.0 | all-reduce | flops 7 | bytes 56 | tf_op jit(solution)/shard_map/psum | solution.py:14
  567.1 8.9 %fusion.54 = f32[2,512,512]{1,2,0:T(8,128)} fusion(bf16[2,8,128,512]{3,2,1,0:T(8,128)(2,1)S(1)} %copy-done, bf16[2,8,512,512]{3,2,1,0:T(8,128)(2,1)} %all-gather.2.cloned.1.call-done, f32[2,128,512]{1,2,0:T(8,128)} %subtract_divide_fusion.1), kind=kOutput, calls=%fused_computation.36 | convolution fusion | flops 2148663296 | bytes 13107200 | tf_op jit(solution)/shard_map/swba,swbc->sac/dot_general | solution.py:53
  576.0 32.5 %reduce-scatter.21.cloned.1.call-done = f32[2,128,512]{1,2,0:T(8,128)} async-done(((f32[2,512,512]{1,2,0:T(8,128)}), f32[2,128,512]{1,2,0:T(8,128)}) %reduce-scatter.21.cloned.1.call-update) | async-done | bytes 524304 | tf_op jit(solution)/shard_map/reduce_scatter | solution.py:56
  616.0 9.6 %all-reduce.8 = (f32[]{:T(128)}, f32[7]{0:T(128)S(1)}) all-reduce(f32[]{:T(128)} %get-tuple-element.198, f32[7]{0:T(128)S(1)} %stack.162), channel_id=1, replica_groups=mesh['grp'=8,'row'=4] {'row'}, use_global_device_ids=true, to_apply=%region_80.0 | all-reduce | flops 8 | bytes 64 | tf_op jit(solution)/shard_map/psum | solution.py:14
  625.7 14.8 %all-reduce.1 = (f32[]{:T(128)}, f32[7]{0:T(128)S(1)}) all-reduce(f32[]{:T(128)} %get-tuple-element.243, f32[7]{0:T(128)S(1)} %get-tuple-element.244), channel_id=1, replica_groups=mesh['grp'=8,'row'=4] {'grp'}, use_global_device_ids=true, to_apply=%region_81.0 | all-reduce | flops 8 | bytes 64 | tf_op jit(solution)/shard_map/psum | solution.py:14
  650.4 8.9 %fusion.59 = f32[2,512,512]{1,2,0:T(8,128)} fusion(bf16[2,8,128,512]{3,2,1,0:T(8,128)(2,1)S(1)} %copy-done, bf16[2,8,512,512]{3,2,1,0:T(8,128)(2,1)} %all-gather.2.cloned.1.call-done, f32[2,128,512]{1,2,0:T(8,128)} %subtract_divide_fusion), kind=kOutput, calls=%fused_computation.38 | convolution fusion | flops 2148663296 | bytes 13107200 | tf_op jit(solution)/shard_map/swba,swbc->sac/dot_general | solution.py:53
  701.6 8.9 %psum.246 = f32[8]{0:T(128)S(1)} all-reduce(f32[8]{0:T(128)S(1)} %stack.171), channel_id=1, replica_groups=mesh['grp'=8,'row'=4] {'row'}, use_global_device_ids=true, to_apply=%region_92.0 | all-reduce | flops 8 | bytes 64 | tf_op jit(solution)/shard_map/psum | solution.py:14
  710.7 14.2 %psum.247 = f32[8,1]{1,0:T(8,128)S(1)} all-reduce(f32[8,1]{1,0:T(8,128)S(1)} %copy.13), channel_id=1, replica_groups=mesh['grp'=8,'row'=4] {'grp'}, use_global_device_ids=true, to_apply=%region_93.0 | all-reduce | flops 8 | bytes 64 | tf_op jit(solution)/shard_map/psum | solution.py:14
  (143 shorter events, 143.0 us)
Async XLA Ops:
  7.2 93.2 %copy-start = (bf16[2,8,128,512]{3,2,1,0:T(8,128)(2,1)S(1)}, bf16[2,8,128,512]{3,2,1,0:T(8,128)(2,1)}, u32[]{:S(2)}) copy-start(bf16[2,8,128,512]{3,2,1,0:T(8,128)(2,1)} %param.35) | copy-start | bytes 6291460
  7.2 1.2 copy-start.2
  7.2 1.4 copy-start.3
  7.2 93.2 %all-gather.2.cloned.1.call-start = ((), (), s32[]{:S(2)}) async-start(), calls=%async_computation.8 | async-start | bytes 10485760 | tf_op jit(solution)/shard_map/all_gather | solution.py:41
  7.9 136.7 %reduce-scatter.9.cloned.1.call-start = ((), (), s32[]{:S(2)}) async-start(), calls=%async_computation.9 | async-start | bytes 2621440 | tf_op jit(solution)/shard_map/reduce_scatter | solution.py:56
  109.3 106.7 %reduce-scatter.11.cloned.1.call-start = ((), (), s32[]{:S(2)}) async-start(), calls=%async_computation.10 | async-start | bytes 2621440 | tf_op jit(solution)/shard_map/reduce_scatter | solution.py:56
  183.4 107.8 %reduce-scatter.13.cloned.1.call-start = ((), (), s32[]{:S(2)}) async-start(), calls=%async_computation.11 | async-start | bytes 2621440 | tf_op jit(solution)/shard_map/reduce_scatter | solution.py:56
  258.7 109.3 %reduce-scatter.15.cloned.1.call-start = ((), (), s32[]{:S(2)}) async-start(), calls=%async_computation.12 | async-start | bytes 2621440 | tf_op jit(solution)/shard_map/reduce_scatter | solution.py:56
  335.4 111.0 %reduce-scatter.17.cloned.1.call-start = ((), (), s32[]{:S(2)}) async-start(), calls=%async_computation.13 | async-start | bytes 2621440 | tf_op jit(solution)/shard_map/reduce_scatter | solution.py:56
  413.9 112.7 %reduce-scatter.19.cloned.1.call-start = ((), (), s32[]{:S(2)}) async-start(), calls=%async_computation.14 | async-start | bytes 2621440 | tf_op jit(solution)/shard_map/reduce_scatter | solution.py:56
  494.0 114.6 %reduce-scatter.21.cloned.1.call-start = ((), (), s32[]{:S(2)}) async-start(), calls=%async_computation.15 | async-start | bytes 2621440 | tf_op jit(solution)/shard_map/reduce_scatter | solution.py:56
  576.0 115.9 %reduce-scatter.23.cloned.1.call-start = ((), (), s32[]{:S(2)}) async-start(), calls=%async_computation.16 | async-start | bytes 2621440 | tf_op jit(solution)/shard_map/reduce_scatter | solution.py:56
  659.3 3.8 copy-start.8
  659.3 4.5 copy-start.7
  659.3 5.2 copy-start.6
  659.3 5.9 copy-start.5
  659.3 6.6 copy-start.4
  725.0 11.2 %copy-start.1 = (f32[8,8]{1,0:T(8,128)}, f32[8,8]{1,0:T(8,128)S(1)}, u32[]{:S(2)}) copy-start(f32[8,8]{1,0:T(8,128)S(1)} %scatter.74) | copy-start | bytes 772
Sparse Core Ops, SparseCore 0:
  9.9 90.4 all-gather.1
  109.4 35.1 reduce-scatter.8
  183.5 32.3 reduce-scatter.10
  258.8 32.3 reduce-scatter.12
  335.5 32.3 reduce-scatter.14
  414.0 32.3 reduce-scatter.16
  494.1 32.3 reduce-scatter.18
  576.1 32.3 reduce-scatter.20
  659.5 32.3 reduce-scatter.22
